TPU v7x, 32 devices: a whole 2x2x4 slice. The times are simulated.
32 devices in a mesh: gx: 4 (over z), gy: 4 (over y, core), gz: 2 (over x).
Axes of the slice: x: 2, y: 2, z: 4, core: 2. Of those that a mesh axis runs over, the one named last changes fastest.
Arguments:
- node_irreps: bfloat16 [4, 4, 2, 16, 25, 128], P('gx', 'gy', 'gz'), may hold values from -5 to 11
- positions: float32 [4, 4, 2, 3, 16], P('gx', 'gy', 'gz'), may hold values from 0 to 6.8
- send_list: int32 [4, 4, 2, 8], P('gx', 'gy', 'gz'), may hold values from 0 to 15, as said below
- neighbours: int32 [4, 4, 2, 16, 32], P('gx', 'gy', 'gz'), may hold values from 0 to 231
- displacements: float32 [4, 4, 2, 3, 512], P('gx', 'gy', 'gz'), may hold values from -6 to 6
- order_zero: bfloat16 [640, 640], replicated, may hold values from -0.25 to 0.25
- order_one: bfloat16 [512, 1024], replicated, may hold values from -0.25 to 0.25
- order_two: bfloat16 [384, 768], replicated, may hold values from -0.3125 to 0.3125
- reciprocal_triples: int32 [1024, 3], replicated, may hold values from -6 to 6
- reciprocal_filter: float32 [1024, 128], replicated, may hold values from 0.1 to 1
- cotangent: float32 [4, 4, 2, 16, 128], P('gx', 'gy', 'gz'), may hold values from -5 to 11
Outputs:
- updated: bfloat16 [4, 4, 2, 16, 25, 128], P('gx', 'gy', 'gz')
- long_range: float32 [4, 4, 2, 16, 128], P('gx', 'gy', 'gz')
- charge_grad: float32 [4, 4, 2, 16, 128], P('gx', 'gy', 'gz')
- position_grad: float32 [4, 4, 2, 3, 16], P('gx', 'gy', 'gz')
Inputs may be any that keep to these rules, and one draw needn't show every extreme that they name: `send_list`: entries of one block are distinct atoms of that block.
All inputs are finite; a program needn't handle non-finite values.
Results may differ from a plain program's by a relative error of at most 0.0023.
Values may be sent and summed in bfloat16 or wider, within the bound.
No kernel may reach another device: no remote copies, remote signals or barrier semaphores. Data moves between devices by JAX's collectives and lax.ppermute only.
A program may use at most 64 MiB of HBM per device.

v0:
```python
import math
import jax
import jax.numpy as jnp
from jax import lax
from jax.sharding import PartitionSpec as P

highest = lax.Precision.HIGHEST
cell_length = 6.8
planar_floor = 0.25
radial_width = 64.0


def with_halo(block, sides, width):
    for axis, dim in sides:
        count = lax.axis_size(axis)
        forward = [(i, i + 1) for i in range(count - 1)]
        forward.append((count - 1, 0))
        backward = [(target, source) for source, target in forward]
        low = lax.ppermute(
            lax.slice_in_dim(block, block.shape[dim] - width, None, axis=dim), axis, forward
        )
        high = lax.ppermute(lax.slice_in_dim(block, 0, width, axis=dim), axis, backward)
        block = jnp.concatenate([low, block, high], axis=dim)
    return block


def harmonic_slot(degree, signed_order):
    return degree * degree + degree + signed_order


def kept_rows():
    layout = []
    for degree in range(5):
        for signed_order in range(-degree, degree + 1):
            layout.append(harmonic_slot(degree, signed_order))
    return layout


def edge_messages(
    lookup_table, displacement, neighbour_index, order_zero, order_one, order_two, layout
):
    atom_count = neighbour_index.shape[0]
    neighbour_count = neighbour_index.shape[1]
    flat_index = neighbour_index.reshape(-1)
    edge_count = flat_index.shape[0]
    feature_width = lookup_table.shape[2]
    source = lookup_table[flat_index]
    length_squared = jnp.sum(displacement * displacement, axis=0)
    radial = jnp.exp(-length_squared / radial_width) / math.sqrt(neighbour_count)
    planar = jnp.sqrt(
        displacement[0] * displacement[0] + displacement[1] * displacement[1] + planar_floor
    )
    cos_one = displacement[0] / planar
    sin_one = displacement[1] / planar

    def neighbour_sum(values):
        weighted = values * radial[:, None, None]
        return jnp.sum(
            weighted.reshape(atom_count, neighbour_count, values.shape[1], feature_width), axis=1
        )

    collected = {}
    zero_slots = [layout.index(harmonic_slot(degree, 0)) for degree in range(5)]
    zero_input = source[:, zero_slots, :].reshape(edge_count, 5 * feature_width)
    zero_output = jnp.dot(zero_input, order_zero, preferred_element_type=jnp.float32)
    summed_zero_part = neighbour_sum(zero_output.reshape(edge_count, 5, feature_width))
    for degree in range(5):
        collected[harmonic_slot(degree, 0)] = summed_zero_part[:, degree]
    rotations = (
        (1, cos_one, sin_one, order_one),
        (2, cos_one * cos_one - sin_one * sin_one, 2.0 * cos_one * sin_one, order_two),
    )
    for harmonic_order, cosine, sine_term, weight_pair in rotations:
        degrees = list(range(harmonic_order, 5))
        count_of_rows = len(degrees)
        plus_slots = [layout.index(harmonic_slot(degree, harmonic_order)) for degree in degrees]
        minus_slots = [layout.index(harmonic_slot(degree, -harmonic_order)) for degree in degrees]
        plus_part = source[:, plus_slots, :].astype(jnp.float32)
        minus_part = source[:, minus_slots, :].astype(jnp.float32)
        cosine_wide = cosine[:, None, None]
        sine_wide = sine_term[:, None, None]
        turned_plus = (cosine_wide * plus_part + sine_wide * minus_part).astype(jnp.bfloat16)
        turned_minus = (cosine_wide * minus_part - sine_wide * plus_part).astype(jnp.bfloat16)
        split_at = count_of_rows * feature_width
        stacked = jnp.concatenate(
            [turned_plus.reshape(edge_count, split_at), turned_minus.reshape(edge_count, split_at)],
            axis=0,
        )
        product = jnp.dot(stacked, weight_pair, preferred_element_type=jnp.float32)
        upper_half = product[:edge_count]
        lower_half = product[edge_count:]
        mixed_plus = (upper_half[:, :split_at] - lower_half[:, split_at:]).reshape(
            edge_count, count_of_rows, feature_width
        )
        mixed_minus = (upper_half[:, split_at:] + lower_half[:, :split_at]).reshape(
            edge_count, count_of_rows, feature_width
        )
        back_plus = neighbour_sum(cosine_wide * mixed_plus - sine_wide * mixed_minus)
        back_minus = neighbour_sum(sine_wide * mixed_plus + cosine_wide * mixed_minus)
        for position_in, degree in enumerate(degrees):
            collected[harmonic_slot(degree, harmonic_order)] = back_plus[:, position_in]
            collected[harmonic_slot(degree, -harmonic_order)] = back_minus[:, position_in]
    zero_block = jnp.zeros((atom_count, feature_width), jnp.float32)
    return jnp.stack([collected.get(slot_number, zero_block) for slot_number in range(25)], axis=1)


def table_product(table, values):
    return jnp.dot(table.T, values, precision=highest)


def local(
    node_irreps,
    positions,
    send_list,
    neighbours,
    displacements,
    order_zero,
    order_one,
    order_two,
    reciprocal_triples,
    reciprocal_filter,
    cotangent,
):
    local_irreps = node_irreps[0, 0, 0]
    atom_count = local_irreps.shape[0]
    size_x = lax.axis_size("gx")
    size_y = lax.axis_size("gy")
    size_z = lax.axis_size("gz")
    total_atom_count = atom_count * size_x * size_y * size_z
    scale_factor = 1.0 / math.sqrt(total_atom_count * reciprocal_filter.shape[0])
    corner = jnp.stack([lax.axis_index("gx"), lax.axis_index("gy"), lax.axis_index("gz")]).astype(
        jnp.float32
    )
    box = cell_length * jnp.array([size_x, size_y, size_z], jnp.float32)
    fractional = (positions[0, 0, 0] + cell_length * corner[:, None]) / box[:, None]
    wave_float = reciprocal_triples.astype(jnp.float32)
    phase = 2.0 * math.pi * jnp.dot(fractional.T, wave_float.T, precision=highest)
    cos_table = jnp.cos(phase)
    sin_table = jnp.sin(phase)
    charges = local_irreps[:, 0, :].astype(jnp.float32)
    grad_input = cotangent[0, 0, 0]
    raw_cos, raw_sin, charge_total, plane_cos, plane_sin = lax.psum(
        (
            table_product(cos_table, charges),
            table_product(sin_table, charges),
            jnp.sum(charges, axis=0),
            jnp.sum(cos_table, axis=0),
            jnp.sum(sin_table, axis=0),
        ),
        ("gx", "gy", "gz"),
    )
    resp_cos, resp_sin = lax.psum(
        (table_product(cos_table, grad_input), table_product(sin_table, grad_input)),
        ("gx", "gy", "gz"),
    )
    mean_charge = charge_total / total_atom_count
    centered = charges - mean_charge
    struct_cos = raw_cos - plane_cos[:, None] * mean_charge[None, :]
    struct_sin = raw_sin - plane_sin[:, None] * mean_charge[None, :]
    sent_rows = send_list[0, 0, 0]
    layout = kept_rows()
    arrived = with_halo(
        local_irreps[sent_rows][None, None, None], (("gx", 0), ("gy", 1), ("gz", 2)), 1
    )
    ghost_table = arrived.reshape((-1,) + local_irreps.shape[1:])
    lookup_table = jnp.concatenate([local_irreps, ghost_table], axis=0)
    messages = edge_messages(
        lookup_table,
        displacements[0, 0, 0],
        neighbours[0, 0, 0],
        order_zero,
        order_one,
        order_two,
        layout,
    )
    updated = (local_irreps.astype(jnp.float32) + messages).astype(jnp.bfloat16)
    long_range = scale_factor * (
        jnp.dot(cos_table, reciprocal_filter * struct_cos, precision=highest)
        + jnp.dot(sin_table, reciprocal_filter * struct_sin, precision=highest)
    )
    charge_term = scale_factor * (
        jnp.dot(cos_table, reciprocal_filter * resp_cos, precision=highest)
        + jnp.dot(sin_table, reciprocal_filter * resp_sin, precision=highest)
    )
    term_mean = (
        scale_factor
        * (
            jnp.dot(plane_cos, reciprocal_filter * resp_cos, precision=highest)
            + jnp.dot(plane_sin, reciprocal_filter * resp_sin, precision=highest)
        )
        / total_atom_count
    )
    charge_grad = charge_term - term_mean
    with_sin = jnp.dot(grad_input, (reciprocal_filter * struct_sin).T, precision=highest) + jnp.dot(
        centered, (reciprocal_filter * resp_sin).T, precision=highest
    )
    with_cos = jnp.dot(grad_input, (reciprocal_filter * struct_cos).T, precision=highest) + jnp.dot(
        centered, (reciprocal_filter * resp_cos).T, precision=highest
    )
    phase_grad = scale_factor * (cos_table * with_sin - sin_table * with_cos)
    position_grad = (2.0 * math.pi * jnp.dot(phase_grad, wave_float, precision=highest) / box).T
    return (
        updated[None, None, None],
        long_range[None, None, None],
        charge_grad[None, None, None],
        position_grad[None, None, None],
    )


def solution(mesh):
    return jax.shard_map(
        local,
        mesh=mesh,
        in_specs=(
            P("gx", "gy", "gz", None, None, None),
            P("gx", "gy", "gz", None, None),
            P("gx", "gy", "gz", None),
            P("gx", "gy", "gz", None, None),
            P("gx", "gy", "gz", None, None),
            P(),
            P(),
            P(),
            P(),
            P(),
            P("gx", "gy", "gz", None, None),
        ),
        out_specs=(
            P("gx", "gy", "gz", None, None, None),
            P("gx", "gy", "gz", None, None),
            P("gx", "gy", "gz", None, None),
            P("gx", "gy", "gz", None, None),
        ),
        check_vma=False,
    )
```

profile of v0, /device:TPU:0, one launch (start us, length us, event | category | flops | bytes accessed | tf_op | source)
XLA Modules:
  0.0 176.4 jit_solution(5121559690905927124)
XLA Ops:
  9.5 5.1 %collective-permute-start.1 = (bf16[1,1,1,8,25,128]{5,4,3,2,1,0:T(8,128)(2,1)S(1)}, bf16[1,1,1,8,25,128]{5,4,3,2,1,0:T(8,128)(2,1)S(1)}, u32[]{:S(2)}, u32[]{:S(2)}) collective-permute-start(bf16[1,1,1,8,25,128]{5,4,3,2,1,0:T(8,128)(2,1)S(1)} %bitcast.173), channel_id=1, source_target_pairs={{8,0},{16,8},{24,16},{0,24},{9,1},{17,9},{25,17},{1,25},{10,2},{18... | collective-permute-start | bytes 153608 | tf_op jit(solution)/shard_map/ppermute | solution.py:22
  14.7 1.3 fusion.62
  16.1 1.4 fusion.40
  17.5 1.4 fusion.42
  18.9 2.5 %fusion.34 = f32[1024,128]{1,0:T(8,128)} fusion(f32[16,1024]{1,0:T(8,128)S(1)} %get-tuple-element.43, f32[1,1,1,16,128]{4,3,2,1,0:T(8,128)} %param.27), kind=kOutput, calls=%fused_computation.112 | convolution fusion | flops 25165824 | bytes 598016 | tf_op jit(solution)/shard_map/dot_general | solution.py:108
  21.4 1.8 %fusion.36 = f32[1024,128]{1,0:T(8,128)} fusion(f32[16,1024]{1,0:T(8,128)S(1)} %get-tuple-element.44, f32[1,1,1,16,128]{4,3,2,1,0:T(8,128)S(1)} %copy-done.11), kind=kOutput, calls=%fused_computation.114 | convolution fusion | flops 25165824 | bytes 598016 | tf_op jit(solution)/shard_map/dot_general | solution.py:108
  23.5 40.4 %all-reduce = (f32[128]{0:T(128)S(1)}, f32[1024]{0:T(1024)S(1)}, f32[1024]{0:T(1024)S(1)}) all-reduce(f32[128]{0:T(128)S(1)} %get-tuple-element.33, f32[1024]{0:T(1024)S(1)} %reduce_sum.87, f32[1024]{0:T(1024)S(1)} %reduce_sum.89), channel_id=1, replica_groups=mesh['gx'=4,'gy'=4,'gz'=2] {'gx','gy','gz'}, use_global_device_ids=true, to_apply=%region_10.0 | all-reduce | flops 2176 | bytes 17408 | tf_op jit(solution)/shard_map/psum | solution.py:142
  64.5 3.0 %collective-permute-done.3 = bf16[3,1,1,8,25,128]{5,4,3,2,1,0:T(8,128)(2,1)S(1)} collective-permute-done((bf16[3,1,1,8,25,128]{5,4,3,2,1,0:T(8,128)(2,1)S(1)}, bf16[3,1,1,8,25,128]{5,4,3,2,1,0:T(8,128)(2,1)S(1)}, u32[]{:S(2)}, u32[]{:S(2)}) %collective-permute-start.3) | collective-permute-done | bytes 153632 | tf_op jit(solution)/shard_map/ppermute | solution.py:22
  67.5 4.2 %collective-permute-done.2 = bf16[3,1,1,8,25,128]{5,4,3,2,1,0:T(8,128)(2,1)S(1)} collective-permute-done((bf16[3,1,1,8,25,128]{5,4,3,2,1,0:T(8,128)(2,1)S(1)}, bf16[3,1,1,8,25,128]{5,4,3,2,1,0:T(8,128)(2,1)S(1)}, u32[]{:S(2)}, u32[]{:S(2)}) %collective-permute-start.2) | collective-permute-done | bytes 153632 | tf_op jit(solution)/shard_map/ppermute | solution.py:19
  74.3 1.5 copy.58
  77.1 8.9 %collective-permute-done.5 = bf16[3,3,1,8,25,128]{5,3,4,2,1,0:T(8,128)(2,1)} collective-permute-done((bf16[3,3,1,8,25,128]{5,3,4,2,1,0:T(8,128)(2,1)S(1)}, bf16[3,3,1,8,25,128]{5,3,4,2,1,0:T(8,128)(2,1)}, u32[]{:S(2)}, u32[]{:S(2)}) %collective-permute-start.5) | collective-permute-done | bytes 460832 | tf_op jit(solution)/shard_map/ppermute | solution.py:22
  87.1 8.1 %collective-permute-done.4 = bf16[3,3,1,8,25,128]{5,3,4,2,1,0:T(8,128)(2,1)} collective-permute-done((bf16[3,3,1,8,25,128]{5,3,4,2,1,0:T(8,128)(2,1)S(1)}, bf16[3,3,1,8,25,128]{5,3,4,2,1,0:T(8,128)(2,1)}, u32[]{:S(2)}, u32[]{:S(2)}) %collective-permute-start.4) | collective-permute-done | bytes 460832 | tf_op jit(solution)/shard_map/ppermute | solution.py:19
  96.9 3.5 %gather_fusion.1 = bf16[512,25,128]{2,1,0:T(8,128)(2,1)} fusion(bf16[232,25,128]{2,1,0:T(8,128)(2,1)S(1)} %pad_maximum_fusion, s32[1024]{0:T(1024)S(1)} %get-tuple-element.75), kind=kCustom, calls=%fused_computation.1 | custom fusion | bytes 6555648 | tf_op jit(solution)/shard_map/gather | solution.py:47
  100.3 5.2 %copy.56 = bf16[512,25,128]{2,0,1:T(8,128)(2,1)} copy(bf16[512,25,128]{2,1,0:T(8,128)(2,1)} %gather_fusion.1) | data formatting | bytes 6553600 | tf_op jit(solution)/shard_map/gather | solution.py:47
  105.5 3.3 %gather_fusion.6 = bf16[3,512,128]{2,1,0:T(8,128)(2,1)} fusion(bf16[512,25,128]{2,0,1:T(8,128)(2,1)} %copy.56, s32[1024]{0:T(1024)S(1)} %get-tuple-element.70), kind=kCustom, calls=%fused_computation.6 | custom fusion | bytes 786444 | tf_op jit(solution)/shard_map/gather | solution.py:79
  108.8 2.5 %gather_fusion.5 = bf16[3,512,128]{2,1,0:T(8,128)(2,1)S(1)} fusion(bf16[512,25,128]{2,0,1:T(8,128)(2,1)} %copy.56, s32[1024]{0:T(1024)S(1)} %get-tuple-element.71), kind=kCustom, calls=%fused_computation.5 | custom fusion | bytes 786444 | tf_op jit(solution)/shard_map/gather | solution.py:78
  113.9 3.4 %gather_fusion.4 = bf16[4,512,128]{2,1,0:T(8,128)(2,1)} fusion(bf16[512,25,128]{2,0,1:T(8,128)(2,1)} %copy.56, s32[1024]{0:T(1024)S(1)} %get-tuple-element.72), kind=kCustom, calls=%fused_computation.4 | custom fusion | bytes 1048592 | tf_op jit(solution)/shard_map/gather | solution.py:79
  117.3 3.4 %gather_fusion.3 = bf16[4,512,128]{2,1,0:T(8,128)(2,1)} fusion(bf16[512,25,128]{2,0,1:T(8,128)(2,1)} %copy.56, s32[1024]{0:T(1024)S(1)} %get-tuple-element.73), kind=kCustom, calls=%fused_computation.3 | custom fusion | bytes 1048592 | tf_op jit(solution)/shard_map/gather | solution.py:78
  120.7 2.6 %gather_fusion.2 = bf16[5,512,128]{2,1,0:T(8,128)(2,1)S(1)} fusion(bf16[512,25,128]{2,0,1:T(8,128)(2,1)} %copy.56, s32[1024]{0:T(1024)S(1)} %get-tuple-element.74), kind=kCustom, calls=%fused_computation.2 | custom fusion | bytes 1310740 | tf_op jit(solution)/shard_map/gather | solution.py:64
  124.4 2.2 %bitcast_reduce_fusion = f32[16,5,128]{2,0,1:T(8,128)S(1)} fusion(f32[512]{0:T(512)S(1)} %exponential_multiply_fusion, bf16[512,640,1]{0,1,2:T(8,128)(2,1)} %bitcast.182, bf16[5,128,640]{2,1,0:T(8,128)(2,1)} %bitcast.181), kind=kOutput, calls=%fused_computation.10 | convolution fusion | flops 420075520 | bytes 1517568 | tf_op jit(solution)/shard_map/dot_general | solution.py:65
  126.7 1.3 copy.61
  129.1 1.3 copy.63
  130.5 1.4 fusion.26
  134.3 1.5 reshape.294
  135.8 3.1 %multiply_reduce_fusion = (f32[16,3,128]{2,1,0:T(4,128)S(1)}, f32[16,3,128]{2,1,0:T(4,128)S(1)}) fusion(f32[16,32,3,128]{3,2,1,0:T(4,128)S(1)} %reshape.294, f32[16,32,3,128]{3,2,1,0:T(4,128)S(1)} %reshape.293, f32[16,32]{1,0:T(8,128)S(1)} %div.88, f32[16,32]{1,0:T(8,128)} %get-tuple-element.60, f32[16,32]{1,0:T(8,128)} %get-tuple-element.59), kind=kLoop, calls=%fused_computation.50 | loop fusion | flops 1953792 | bytes 1628160 | tf_op jit(solution)/shard_map/reduce_sum | solution.py:58
  140.6 1.8 %slice_subtract_fusion = (f32[512,512]{1,0:T(8,128)}, f32[512,512]{1,0:T(8,128)}) fusion(f32[1024,1024]{1,0:T(8,128)S(1)} %fusion.13), kind=kLoop, calls=%fused_computation.35 | loop fusion | flops 524288 | bytes 6291456 | tf_op jit(solution)/shard_map/sub | solution.py:92
  142.4 1.6 reshape.291
  144.1 2.6 %reshape.292 = f32[16,32,4,128]{3,2,1,0:T(4,128)} reshape(f32[512,512]{1,0:T(8,128)} %get-tuple-element.36) | data formatting | bytes 2097152 | tf_op jit(solution)/shard_map/reshape | solution.py:95
  146.7 3.7 %multiply_reduce_fusion.2 = (f32[16,4,128]{2,1,0:T(4,128)S(1)}, f32[16,4,128]{2,1,0:T(4,128)S(1)}) fusion(f32[16,32,4,128]{3,2,1,0:T(4,128)} %reshape.292, f32[16,32,4,128]{3,2,1,0:T(4,128)S(1)} %reshape.291, f32[16,32]{1,0:T(8,128)S(1)} %div.88, f32[16,32]{1,0:T(8,128)S(1)} %copy-done.13, f32[16,32]{1,0:T(8,128)S(1)} %copy-done.14), kind=kLoop, calls=%fused_computation.52 | loop fusion | flops 2605056 | bytes 2168832 | tf_op jit(solution)/shard_map/reduce_sum | solution.py:58
  151.3 8.9 %all-reduce.4.cloned.1.call-done = (f32[1024,128]{1,0:T(8,128)}, f32[1024,128]{1,0:T(8,128)}, f32[1024,128]{1,0:T(8,128)}, f32[1024,128]{1,0:T(8,128)}) async-done(((f32[1024,128]{1,0:T(8,128)}, f32[1024,128]{1,0:T(8,128)}, f32[1024,128]{1,0:T(8,128)}, f32[1024,128]{1,0:T(8,128)}), (f32[1024,128]{1,0:T(8,128)}, f32[1024,128]{1,0:T(8,128)}, f32[1024,128]{1,0:T(8,128)}, ...) | async-done | bytes 2097168 | tf_op jit(solution)/shard_map/psum | solution.py:142
  160.3 1.6 fusion.29
  161.8 1.7 convolution_bitcast_fusion
  (143 shorter events, 25.5 us)
Async XLA Ops:
  7.2 132.1 %copy-start = (bf16[512,1024]{1,0:T(8,128)(2,1)S(1)}, bf16[512,1024]{1,0:T(8,128)(2,1)}, u32[]{:S(2)}) copy-start(bf16[512,1024]{1,0:T(8,128)(2,1)} %param.23) | copy-start | bytes 3145732
  7.2 14.2 %copy-start.11 = (f32[1,1,1,16,128]{4,3,2,1,0:T(8,128)S(1)}, f32[1,1,1,16,128]{4,3,2,1,0:T(8,128)}, u32[]{:S(2)}) copy-start(f32[1,1,1,16,128]{4,3,2,1,0:T(8,128)} %param.27) | copy-start | bytes 24580
  7.2 153.1 %all-reduce.4.cloned.1.call-start = ((), (), s32[]{:S(2)}) async-start(), calls=%async_computation | async-start | bytes 4194304 | tf_op jit(solution)/shard_map/psum | solution.py:142
  9.5 54.4 %collective-permute-start.1 = (bf16[1,1,1,8,25,128]{5,4,3,2,1,0:T(8,128)(2,1)S(1)}, bf16[1,1,1,8,25,128]{5,4,3,2,1,0:T(8,128)(2,1)S(1)}, u32[]{:S(2)}, u32[]{:S(2)}) collective-permute-start(bf16[1,1,1,8,25,128]{5,4,3,2,1,0:T(8,128)(2,1)S(1)} %bitcast.173), channel_id=1, source_target_pairs={{8,0},{16,8},{24,16},{0,24},{9,1},{17,9},{25,17},{1,25},{10,2},{18... | collective-permute-start | bytes 153608 | tf_op jit(solution)/shard_map/ppermute | solution.py:22
  14.6 49.3 %collective-permute-start = (bf16[1,1,1,8,25,128]{5,4,3,2,1,0:T(8,128)(2,1)S(1)}, bf16[1,1,1,8,25,128]{5,4,3,2,1,0:T(8,128)(2,1)S(1)}, u32[]{:S(2)}, u32[]{:S(2)}) collective-permute-start(bf16[1,1,1,8,25,128]{5,4,3,2,1,0:T(8,128)(2,1)S(1)} %bitcast.174), channel_id=1, source_target_pairs={{0,8},{8,16},{16,24},{24,0},{1,9},{9,17},{17,25},{25,1},{2,10},{10... | collective-permute-start | bytes 153608 | tf_op jit(solution)/shard_map/ppermute | solution.py:19
  17.5 5.8 %copy-start.15 = (f32[1,1,1,3,512]{4,2,3,1,0:T(1,128)S(1)}, f32[1,1,1,3,512]{4,2,3,1,0:T(1,128)}, u32[]{:S(2)}) copy-start(f32[1,1,1,3,512]{4,2,3,1,0:T(1,128)} %param.21) | copy-start | bytes 18436
  17.5 5.9 %copy-start.20 = (s32[1,1,1,16,32]{4,3,2,1,0:T(8,128)S(1)}, s32[1,1,1,16,32]{4,3,2,1,0:T(8,128)}, u32[]{:S(2)}) copy-start(s32[1,1,1,16,32]{4,3,2,1,0:T(8,128)} %param.20) | copy-start | bytes 6148
  18.9 45.6 %copy-start.26 = (s32[5]{0:T(128)S(1)}, s32[5]{0:T(128)}, u32[]{:S(2)}) copy-start(s32[5]{0:T(128)} %constant.102) | copy-start | bytes 64
  18.9 45.6 %copy-start.24 = (s32[4]{0:T(128)S(1)}, s32[4]{0:T(128)}, u32[]{:S(2)}) copy-start(s32[4]{0:T(128)} %constant.104) | copy-start | bytes 52
  18.9 45.7 %copy-start.25 = (s32[4]{0:T(128)S(1)}, s32[4]{0:T(128)}, u32[]{:S(2)}) copy-start(s32[4]{0:T(128)} %constant.103) | copy-start | bytes 52
  23.2 50.8 %copy-start.22 = (s32[3]{0:T(128)S(1)}, s32[3]{0:T(128)}, u32[]{:S(2)}) copy-start(s32[3]{0:T(128)} %constant.106) | copy-start | bytes 40
  23.3 50.8 %copy-start.23 = (s32[3]{0:T(128)S(1)}, s32[3]{0:T(128)}, u32[]{:S(2)}) copy-start(s32[3]{0:T(128)} %constant.105) | copy-start | bytes 40
  23.3 51.1 %copy-start.8 = (bf16[640,640]{1,0:T(8,128)(2,1)S(1)}, bf16[640,640]{1,0:T(8,128)(2,1)}, u32[]{:S(2)}) copy-start(bf16[640,640]{1,0:T(8,128)(2,1)} %param.22) | copy-start | bytes 2457604
  63.9 3.6 %collective-permute-start.3 = (bf16[3,1,1,8,25,128]{5,4,3,2,1,0:T(8,128)(2,1)S(1)}, bf16[3,1,1,8,25,128]{5,4,3,2,1,0:T(8,128)(2,1)S(1)}, u32[]{:S(2)}, u32[]{:S(2)}) collective-permute-start(bf16[3,1,1,8,25,128]{5,4,3,2,1,0:T(8,128)(2,1)S(1)} %pad_maximum_fusion.3), channel_id=1, source_target_pairs={{2,0},{4,2},{6,4},{0,6},{3,1},{5,3},{7,5},{1,7},{10,8},{12,10},{14... | collective-permute-start | bytes 460808 | tf_op jit(solution)/shard_map/ppermute | solution.py:22
  64.0 7.7 %collective-permute-start.2 = (bf16[3,1,1,8,25,128]{5,4,3,2,1,0:T(8,128)(2,1)S(1)}, bf16[3,1,1,8,25,128]{5,4,3,2,1,0:T(8,128)(2,1)S(1)}, u32[]{:S(2)}, u32[]{:S(2)}) collective-permute-start(bf16[3,1,1,8,25,128]{5,4,3,2,1,0:T(8,128)(2,1)S(1)} %pad_maximum_fusion.3), channel_id=1, source_target_pairs={{0,2},{2,4},{4,6},{6,0},{1,3},{3,5},{5,7},{7,1},{8,10},{10,12},{12... | collective-permute-start | bytes 460808 | tf_op jit(solution)/shard_map/ppermute | solution.py:19
  72.0 14.0 %collective-permute-start.5 = (bf16[3,3,1,8,25,128]{5,3,4,2,1,0:T(8,128)(2,1)S(1)}, bf16[3,3,1,8,25,128]{5,3,4,2,1,0:T(8,128)(2,1)}, u32[]{:S(2)}, u32[]{:S(2)}) collective-permute-start(bf16[3,3,1,8,25,128]{5,3,4,2,1,0:T(8,128)(2,1)S(1)} %copy.50), channel_id=1, source_target_pairs={{1,0},{0,1},{3,2},{2,3},{5,4},{4,5},{7,6},{6,7},{9,8},{8,9},{11,10... | collective-permute-start | bytes 1382408 | tf_op jit(solution)/shard_map/ppermute | solution.py:22
  73.0 22.2 %collective-permute-start.4 = (bf16[3,3,1,8,25,128]{5,3,4,2,1,0:T(8,128)(2,1)S(1)}, bf16[3,3,1,8,25,128]{5,3,4,2,1,0:T(8,128)(2,1)}, u32[]{:S(2)}, u32[]{:S(2)}) collective-permute-start(bf16[3,3,1,8,25,128]{5,3,4,2,1,0:T(8,128)(2,1)S(1)} %copy.50), channel_id=1, source_target_pairs={{0,1},{1,0},{2,3},{3,2},{4,5},{5,4},{6,7},{7,6},{8,9},{9,8},{10,11... | collective-permute-start | bytes 1382408 | tf_op jit(solution)/shard_map/ppermute | solution.py:19
  124.4 2.2 %copy-start.6 = (bf16[4,512,128]{2,1,0:T(8,128)(2,1)S(1)}, bf16[4,512,128]{2,1,0:T(8,128)(2,1)}, u32[]{:S(2)}) copy-start(bf16[4,512,128]{2,1,0:T(8,128)(2,1)} %gather_fusion.3) | copy-start | bytes 1572868
  128.0 2.5 %copy-start.18 = (f32[512]{0:T(512)S(1)}, f32[512]{0:T(512)}, u32[]{:S(2)}) copy-start(f32[512]{0:T(512)} %get-tuple-element.65) | copy-start | bytes 6148
  128.0 2.5 %copy-start.19 = (f32[512]{0:T(512)S(1)}, f32[512]{0:T(512)}, u32[]{:S(2)}) copy-start(f32[512]{0:T(512)} %get-tuple-element.68) | copy-start | bytes 6148
  135.7 3.2 %copy-start.4 = (f32[512,4,128]{0,2,1:T(8,128)S(1)}, f32[512,4,128]{0,2,1:T(8,128)}, u32[]{:S(2)}) copy-start(f32[512,4,128]{0,2,1:T(8,128)} %copy.61) | copy-start | bytes 3145732
  135.7 3.2 %copy-start.5 = (f32[512,4,128]{0,2,1:T(8,128)S(1)}, f32[512,4,128]{0,2,1:T(8,128)}, u32[]{:S(2)}) copy-start(f32[512,4,128]{0,2,1:T(8,128)} %copy.63) | copy-start | bytes 3145732
  135.8 3.2 %copy-start.16 = (f32[512]{0:T(512)S(1)}, f32[512]{0:T(512)}, u32[]{:S(2)}) copy-start(f32[512]{0:T(512)} %get-tuple-element.66) | copy-start | bytes 6148
  135.8 3.2 %copy-start.17 = (f32[512]{0:T(512)S(1)}, f32[512]{0:T(512)}, u32[]{:S(2)}) copy-start(f32[512]{0:T(512)} %get-tuple-element.67) | copy-start | bytes 6148
  142.4 4.2 %copy-start.13 = (f32[16,32]{1,0:T(8,128)S(1)}, f32[16,32]{1,0:T(8,128)}, u32[]{:S(2)}) copy-start(f32[16,32]{1,0:T(8,128)} %get-tuple-element.61) | copy-start | bytes 6148
  142.4 4.2 %copy-start.14 = (f32[16,32]{1,0:T(8,128)S(1)}, f32[16,32]{1,0:T(8,128)}, u32[]{:S(2)}) copy-start(f32[16,32]{1,0:T(8,128)} %get-tuple-element.62) | copy-start | bytes 6148
  144.0 6.6 %copy-start.10 = (bf16[1,1,1,16,25,128]{5,3,4,2,1,0:T(8,128)(2,1)S(1)}, bf16[1,1,1,16,25,128]{5,3,4,2,1,0:T(8,128)(2,1)}, u32[]{:S(2)}) copy-start(bf16[1,1,1,16,25,128]{5,3,4,2,1,0:T(8,128)(2,1)} %param.17) | copy-start | bytes 307204
  146.6 13.6 %copy-start.1 = (f32[1024,128]{1,0:T(8,128)S(1)}, f32[1024,128]{1,0:T(8,128)}, u32[]{:S(2)}) copy-start(f32[1024,128]{1,0:T(8,128)} %param.26) | copy-start | bytes 1572868
  160.2 3.3 %copy-start.3 = (f32[1024,128]{1,0:T(8,128)S(1)}, f32[1024,128]{1,0:T(8,128)}, u32[]{:S(2)}) copy-start(f32[1024,128]{1,0:T(8,128)} %get-tuple-element.31) | copy-start | bytes 1572868
  164.4 2.4 %copy-start.2 = (f32[1024,128]{1,0:T(8,128)S(1)}, f32[1024,128]{1,0:T(8,128)}, u32[]{:S(2)}) copy-start(f32[1024,128]{1,0:T(8,128)} %get-tuple-element.32) | copy-start | bytes 1572868
  165.0 2.4 %copy-start.12 = (s32[1024,3]{0,1:T(4,128)S(1)}, s32[1024,3]{0,1:T(4,128)}, u32[]{:S(2)}) copy-start(s32[1024,3]{0,1:T(4,128)} %param.25) | copy-start | bytes 36868
  165.0 2.4 %copy-start.21 = (f32[3]{0:T(128)S(1)}, f32[3]{0:T(128)}, u32[]{:S(2)}) copy-start(f32[3]{0:T(128)} %constant.100) | copy-start | bytes 40
  (2 other events, 2.8 us)
Sparse Core Ops, SparseCore 0:
  23.4 136.8 all-reduce.3
where the time goes:
time: 177 us; the launch traced here: 176 us
  local copies, waits for them, and re-layouts  41.7 us (24%)
  blocking collectives  40.4 us (23%)
  waiting for transfers between devices  33.1 us (19%)
  matrix products  21.6 us (12%)
  other arithmetic  17.1 us (10%)
  between operations  14.7 us (8%)
  starting transfers between devices  7.82 us (4%)
    psum x1, blocking collectives, local(): lax.psum((table_product(cos_table, charges), table_product(sin_table, cha...  40.4 us
    ppermute x3, waiting for transfers between devices, with_halo(): lax.ppermute(lax.slice_in_dim(block, block.shape[dim] - width, None, axis...  12.3 us
    ppermute x3, waiting for transfers between devices, with_halo(): lax.ppermute(lax.slice_in_dim(block, 0, width, axis=dim), axis, backward)  11.8 us
    psum x1, waiting for transfers between devices, local(): lax.psum((table_product(cos_table, charges), table_product(sin_table, cha...  8.93 us
    gather x2, local copies, waits for them, and re-layouts, edge_messages(): source = lookup_table[flat_index]  8.67 us
    dot_general x4, matrix products, table_product(): return jnp.dot(table.T, values, precision=highest)  7.14 us
    reduce_sum x2, other arithmetic, neighbour_sum(): jnp.sum(weighted.reshape(atom_count, neighbour_count, values.shape[1], fe...  6.74 us
    gather x2, local copies, waits for them, and re-layouts, edge_messages(): minus_part = source[:, minus_slots, :].astype(jnp.float32)  6.71 us
  transfers between devices with their start and end apart: 7, of which 5 were waited for; matrix products, arithmetic and copies ran while one was open for 39% of the time, Pallas kernels for 0%

commit v1 on v0

--- a/solution.py
+++ b/solution.py
@@ -140,14 +140,17 @@
     charges = local_irreps[:, 0, :].astype(jnp.float32)
     grad_input = cotangent[0, 0, 0]
     raw_cos, raw_sin, charge_total, plane_cos, plane_sin = lax.psum(
-        (
-            table_product(cos_table, charges),
-            table_product(sin_table, charges),
-            jnp.sum(charges, axis=0),
-            jnp.sum(cos_table, axis=0),
-            jnp.sum(sin_table, axis=0),
+        lax.psum(
+            (
+                table_product(cos_table, charges),
+                table_product(sin_table, charges),
+                jnp.sum(charges, axis=0),
+                jnp.sum(cos_table, axis=0),
+                jnp.sum(sin_table, axis=0),
+            ),
+            ("gy", "gz"),
         ),
-        ("gx", "gy", "gz"),
+        "gx",
     )
     resp_cos, resp_sin = lax.psum(
         (table_product(cos_table, grad_input), table_product(sin_table, grad_input)),

time: 177 us -> 288 us (1.63)
  waiting for transfers between devices: 33.1 us -> 148 us
  blocking collectives: 40.4 us -> 27.4 us
  other arithmetic: 17.1 us -> 21.7 us
    psum x0 -> x2, waiting for transfers between devices: none -> 88.2 us  [the longest x1 88.2 us: local(): lax.psum((table_product(cos_table, grad_input), table_product(sin_table,...]
    psum x1, waiting for transfers between devices: 8.93 us -> 54.6 us  [local(): lax.psum((table_product(cos_table, charges), table_product(sin_table, cha...]
    psum x1, blocking collectives: 40.4 us -> 14.4 us  [local(): lax.psum((table_product(cos_table, charges), table_product(sin_table, cha...]
    psum x0 -> x1, blocking collectives: none -> 13 us  [local(): lax.psum(lax.psum((table_product(cos_table, charges), table_product(sin_t...]
    ppermute x3, waiting for transfers between devices: 11.8 us -> 1.67 us  [with_halo(): lax.ppermute(lax.slice_in_dim(block, 0, width, axis=dim), axis, backward)]
    ppermute x3, waiting for transfers between devices: 12.3 us -> 3.24 us  [with_halo(): lax.ppermute(lax.slice_in_dim(block, block.shape[dim] - width, None, axis...]
  transfers between devices with their start and end apart: 7 -> 9, of which waited for: 5 -> 4; matrix products, arithmetic and copies ran while one was open for 39% -> 28% of each run, Pallas kernels for 0% -> 0%
where the time goes in v1:
time: 288 us; the launch traced here: 287 us
  waiting for transfers between devices  148 us (51%)
  local copies, waits for them, and re-layouts  42.9 us (15%)
  blocking collectives  27.4 us (10%)
  matrix products  24.4 us (8%)
  other arithmetic  21.7 us (8%)
  between operations  14.6 us (5%)
  starting transfers between devices  7.9 us (3%)
    psum x1, waiting for transfers between devices, local(): lax.psum((table_product(cos_table, grad_input), table_product(sin_table,...  88.2 us
    psum x1, waiting for transfers between devices, local(): lax.psum((table_product(cos_table, charges), table_product(sin_table, cha...  54.6 us
    psum x1, blocking collectives, local(): lax.psum((table_product(cos_table, charges), table_product(sin_table, cha...  14.4 us
    psum x1, blocking collectives, local(): lax.psum(lax.psum((table_product(cos_table, charges), table_product(sin_t...  13 us
    gather x2, local copies, waits for them, and re-layouts, edge_messages(): source = lookup_table[flat_index]  8.91 us
    dot_general x4, matrix products, table_product(): return jnp.dot(table.T, values, precision=highest)  7.83 us
    reduce_sum x2, other arithmetic, neighbour_sum(): jnp.sum(weighted.reshape(atom_count, neighbour_count, values.shape[1], fe...  7.16 us
    gather x2, local copies, waits for them, and re-layouts, edge_messages(): minus_part = source[:, minus_slots, :].astype(jnp.float32)  6.9 us
  transfers between devices with their start and end apart: 9, of which 4 were waited for; matrix products, arithmetic and copies ran while one was open for 28% of the time, Pallas kernels for 0%

profile of v1, /device:TPU:0, one launch (start us, length us, event | category | flops | bytes accessed | tf_op | source)
XLA Modules:
  0.0 286.6 jit_solution(14387929427936474369)
XLA Ops:
  9.5 5.1 %collective-permute-start.1 = (bf16[1,1,1,8,25,128]{5,4,3,2,1,0:T(8,128)(2,1)S(1)}, bf16[1,1,1,8,25,128]{5,4,3,2,1,0:T(8,128)(2,1)S(1)}, u32[]{:S(2)}, u32[]{:S(2)}) collective-permute-start(bf16[1,1,1,8,25,128]{5,4,3,2,1,0:T(8,128)(2,1)S(1)} %bitcast.173), channel_id=1, source_target_pairs={{8,0},{16,8},{24,16},{0,24},{9,1},{17,9},{25,17},{1,25},{10,2},{18... | collective-permute-start | bytes 153608 | tf_op jit(solution)/shard_map/ppermute | solution.py:22
  16.0 2.5 fusion.34
  18.5 2.5 fusion.36
  21.2 1.4 fusion.40
  22.6 1.4 fusion.42
  24.4 14.4 %all-reduce.1 = (f32[128]{0:T(128)S(1)}, f32[1024]{0:T(1024)S(1)}, f32[1024]{0:T(1024)S(1)}) all-reduce(f32[128]{0:T(128)S(1)} %get-tuple-element.38, f32[1024]{0:T(1024)S(1)} %reduce_sum.87, f32[1024]{0:T(1024)S(1)} %reduce_sum.89), channel_id=1, replica_groups=mesh['gx'=4,'gy'=4,'gz'=2] {'gy','gz'}, use_global_device_ids=true, to_apply=%region_12.0 | all-reduce | flops 2176 | bytes 17408 | tf_op jit(solution)/shard_map/psum | solution.py:143
  38.9 13.0 %all-reduce.3 = (f32[128]{0:T(128)S(1)}, f32[1024]{0:T(1024)S(1)}, f32[1024]{0:T(1024)S(1)}) all-reduce(f32[128]{0:T(128)S(1)} %get-tuple-element.28, f32[1024]{0:T(1024)S(1)} %get-tuple-element.29, f32[1024]{0:T(1024)S(1)} %get-tuple-element.30), channel_id=1, replica_groups=mesh['gx'=4,'gy'=4,'gz'=2] {'gx'}, use_global_device_ids=true, to_apply=%region_13.0 | all-reduce | flops 2176 | bytes 17408 | tf_op jit(solution)/shard_map/psum | solution.py:142
  55.6 1.3 copy.58
  57.5 1.7 collective-permute-done.3
  59.2 3.2 %collective-permute-done.2 = bf16[3,1,1,8,25,128]{5,4,3,2,1,0:T(8,128)(2,1)} collective-permute-done((bf16[3,1,1,8,25,128]{5,4,3,2,1,0:T(8,128)(2,1)S(1)}, bf16[3,1,1,8,25,128]{5,4,3,2,1,0:T(8,128)(2,1)}, u32[]{:S(2)}, u32[]{:S(2)}) %collective-permute-start.2) | collective-permute-done | bytes 153632 | tf_op jit(solution)/shard_map/ppermute | solution.py:19
  64.1 1.7 collective-permute-start.4
  65.7 88.2 %all-reduce.9.cloned.1.call-done = (f32[1024,128]{1,0:T(8,128)}, f32[1024,128]{1,0:T(8,128)}) async-done(((f32[1024,128]{1,0:T(8,128)}, f32[1024,128]{1,0:T(8,128)}), (f32[1024,128]{1,0:T(8,128)}, f32[1024,128]{1,0:T(8,128)})) %all-reduce.9.cloned.1.call-update) | async-done | bytes 1048592 | tf_op jit(solution)/shard_map/psum | solution.py:155
  153.9 1.5 convolution_bitcast_fusion.3
  155.4 1.4 fusion.12
  158.3 54.6 %all-reduce.11.cloned.1.call-done = (f32[1024,128]{1,0:T(8,128)}, f32[1024,128]{1,0:T(8,128)}) async-done(((f32[1024,128]{1,0:T(8,128)}, f32[1024,128]{1,0:T(8,128)}), (f32[1024,128]{1,0:T(8,128)}, f32[1024,128]{1,0:T(8,128)})) %all-reduce.11.cloned.1.call-update) | async-done | bytes 1048592 | tf_op jit(solution)/shard_map/psum | solution.py:143
  215.7 3.6 %gather_fusion.1 = bf16[512,25,128]{2,1,0:T(8,128)(2,1)} fusion(bf16[232,25,128]{2,1,0:T(8,128)(2,1)S(1)} %pad_maximum_fusion, s32[1024]{0:T(1024)} %get-tuple-element.80), kind=kCustom, calls=%fused_computation.1 | custom fusion | bytes 6555648 | tf_op jit(solution)/shard_map/gather | solution.py:47
  219.3 5.3 %copy.56 = bf16[512,25,128]{2,0,1:T(8,128)(2,1)} copy(bf16[512,25,128]{2,1,0:T(8,128)(2,1)} %gather_fusion.1) | data formatting | bytes 6553600 | tf_op jit(solution)/shard_map/gather | solution.py:47
  224.6 3.4 %gather_fusion.6 = bf16[3,512,128]{2,1,0:T(8,128)(2,1)} fusion(bf16[512,25,128]{2,0,1:T(8,128)(2,1)} %copy.56, s32[1024]{0:T(1024)} %get-tuple-element.75), kind=kCustom, calls=%fused_computation.6 | custom fusion | bytes 786444 | tf_op jit(solution)/shard_map/gather | solution.py:79
  228.0 2.7 gather_fusion.5
  233.3 3.5 %gather_fusion.4 = bf16[4,512,128]{2,1,0:T(8,128)(2,1)} fusion(bf16[512,25,128]{2,0,1:T(8,128)(2,1)} %copy.56, s32[1024]{0:T(1024)} %get-tuple-element.77), kind=kCustom, calls=%fused_computation.4 | custom fusion | bytes 1048592 | tf_op jit(solution)/shard_map/gather | solution.py:79
  236.8 3.5 %gather_fusion.3 = bf16[4,512,128]{2,1,0:T(8,128)(2,1)} fusion(bf16[512,25,128]{2,0,1:T(8,128)(2,1)} %copy.56, s32[1024]{0:T(1024)} %get-tuple-element.78), kind=kCustom, calls=%fused_computation.3 | custom fusion | bytes 1048592 | tf_op jit(solution)/shard_map/gather | solution.py:78
  240.2 2.7 gather_fusion.2
  244.0 2.2 bitcast_reduce_fusion
  250.7 1.4 fusion.26
  254.2 1.5 reshape.293
  257.0 3.8 %multiply_reduce_fusion = (f32[16,3,128]{2,1,0:T(4,128)S(1)}, f32[16,3,128]{2,1,0:T(4,128)S(1)}) fusion(f32[16,32,3,128]{3,2,1,0:T(4,128)} %reshape.294, f32[16,32,3,128]{3,2,1,0:T(4,128)S(1)} %reshape.293, f32[16,32]{1,0:T(8,128)S(1)} %div.88, f32[16,32]{1,0:T(8,128)S(1)} %copy-done.25, f32[16,32]{1,0:T(8,128)S(1)} %copy-done.24), kind=kLoop, calls=%fused_computation.50 | loop fusion | flops 1953792 | bytes 1628160 | tf_op jit(solution)/shard_map/reduce_sum | solution.py:58
  262.5 1.8 slice_subtract_fusion
  264.3 1.6 reshape.291
  265.9 2.6 reshape.292
  268.6 3.4 %multiply_reduce_fusion.2 = (f32[16,4,128]{2,1,0:T(4,128)S(1)}, f32[16,4,128]{2,1,0:T(4,128)S(1)}) fusion(f32[16,32,4,128]{3,2,1,0:T(4,128)} %reshape.292, f32[16,32,4,128]{3,2,1,0:T(4,128)S(1)} %reshape.291, f32[16,32]{1,0:T(8,128)S(1)} %div.88, f32[16,32]{1,0:T(8,128)S(1)} %copy-done.22, f32[16,32]{1,0:T(8,128)S(1)} %copy-done.23), kind=kLoop, calls=%fused_computation.52 | loop fusion | flops 2605056 | bytes 2168832 | tf_op jit(solution)/shard_map/reduce_sum | solution.py:58
  273.0 1.6 fusion.29
  274.6 1.8 convolution_bitcast_fusion
  (178 shorter events, 31.8 us)
Async XLA Ops:
  7.2 254.0 %copy-start = (bf16[512,1024]{1,0:T(8,128)(2,1)S(1)}, bf16[512,1024]{1,0:T(8,128)(2,1)}, u32[]{:S(2)}) copy-start(bf16[512,1024]{1,0:T(8,128)(2,1)} %param.23) | copy-start | bytes 3145732
  7.2 146.7 %all-reduce.9.cloned.1.call-start = ((), (), s32[]{:S(2)}) async-start(), calls=%async_computation | async-start | bytes 2097152 | tf_op jit(solution)/shard_map/psum | solution.py:155
  8.9 15.1 %copy-start.12 = (bf16[1,1,1,16,25,128]{5,4,3,2,1,0:T(8,128)(2,1)}, bf16[1,1,1,16,25,128]{5,4,3,2,1,0:T(8,128)(2,1)S(1)}, u32[]{:S(2)}) copy-start(bf16[1,1,1,16,25,128]{5,4,3,2,1,0:T(8,128)(2,1)S(1)} %copy.82) | copy-start | bytes 307204
  9.5 44.8 %collective-permute-start.1 = (bf16[1,1,1,8,25,128]{5,4,3,2,1,0:T(8,128)(2,1)S(1)}, bf16[1,1,1,8,25,128]{5,4,3,2,1,0:T(8,128)(2,1)S(1)}, u32[]{:S(2)}, u32[]{:S(2)}) collective-permute-start(bf16[1,1,1,8,25,128]{5,4,3,2,1,0:T(8,128)(2,1)S(1)} %bitcast.173), channel_id=1, source_target_pairs={{8,0},{16,8},{24,16},{0,24},{9,1},{17,9},{25,17},{1,25},{10,2},{18... | collective-permute-start | bytes 153608 | tf_op jit(solution)/shard_map/ppermute | solution.py:22
  14.6 39.7 %collective-permute-start = (bf16[1,1,1,8,25,128]{5,4,3,2,1,0:T(8,128)(2,1)S(1)}, bf16[1,1,1,8,25,128]{5,4,3,2,1,0:T(8,128)(2,1)S(1)}, u32[]{:S(2)}, u32[]{:S(2)}) collective-permute-start(bf16[1,1,1,8,25,128]{5,4,3,2,1,0:T(8,128)(2,1)S(1)} %bitcast.174), channel_id=1, source_target_pairs={{0,8},{8,16},{16,24},{24,0},{1,9},{9,17},{17,25},{25,1},{2,10},{10... | collective-permute-start | bytes 153608 | tf_op jit(solution)/shard_map/ppermute | solution.py:19
  16.0 141.3 %copy-start.8 = (f32[16,1024]{1,0:T(8,128)}, f32[16,1024]{1,0:T(8,128)S(1)}, u32[]{:S(2)}) copy-start(f32[16,1024]{1,0:T(8,128)S(1)} %get-tuple-element.48) | copy-start | bytes 196612
  18.5 5.5 %copy-start.27 = (f32[1,1,1,3,512]{4,2,3,1,0:T(1,128)S(1)}, f32[1,1,1,3,512]{4,2,3,1,0:T(1,128)}, u32[]{:S(2)}) copy-start(f32[1,1,1,3,512]{4,2,3,1,0:T(1,128)} %param.21) | copy-start | bytes 18436
  18.5 5.6 %copy-start.32 = (s32[1,1,1,16,32]{4,3,2,1,0:T(8,128)S(1)}, s32[1,1,1,16,32]{4,3,2,1,0:T(8,128)}, u32[]{:S(2)}) copy-start(s32[1,1,1,16,32]{4,3,2,1,0:T(8,128)} %param.20) | copy-start | bytes 6148
  21.1 32.6 %copy-start.40 = (s32[5]{0:T(128)S(1)}, s32[5]{0:T(128)}, u32[]{:S(2)}) copy-start(s32[5]{0:T(128)} %constant.102) | copy-start | bytes 64
  21.1 33.8 %copy-start.38 = (s32[4]{0:T(128)S(1)}, s32[4]{0:T(128)}, u32[]{:S(2)}) copy-start(s32[4]{0:T(128)} %constant.104) | copy-start | bytes 52
  21.1 33.8 %copy-start.39 = (s32[4]{0:T(128)S(1)}, s32[4]{0:T(128)}, u32[]{:S(2)}) copy-start(s32[4]{0:T(128)} %constant.103) | copy-start | bytes 52
  21.1 34.5 %copy-start.14 = (bf16[640,640]{1,0:T(8,128)(2,1)S(1)}, bf16[640,640]{1,0:T(8,128)(2,1)}, u32[]{:S(2)}) copy-start(bf16[640,640]{1,0:T(8,128)(2,1)} %param.22) | copy-start | bytes 2457604
  21.1 191.8 %all-reduce.11.cloned.1.call-start = ((), (), s32[]{:S(2)}) async-start(), calls=%async_computation.1 | async-start | bytes 2097152 | tf_op jit(solution)/shard_map/psum | solution.py:143
  22.6 34.3 %copy-start.36 = (s32[3]{0:T(128)S(1)}, s32[3]{0:T(128)}, u32[]{:S(2)}) copy-start(s32[3]{0:T(128)} %constant.106) | copy-start | bytes 40
  22.6 34.3 %copy-start.37 = (s32[3]{0:T(128)S(1)}, s32[3]{0:T(128)}, u32[]{:S(2)}) copy-start(s32[3]{0:T(128)} %constant.105) | copy-start | bytes 40
  24.0 249.0 %all-reduce.13.cloned.1.call-start = ((), (), s32[]{:S(2)}) async-start(), calls=%async_computation.2 | async-start | bytes 2097152 | tf_op jit(solution)/shard_map/psum | solution.py:142
  24.3 39.4 %copy-start.33 = (f32[512]{0:T(512)}, f32[512]{0:T(512)S(1)}, u32[]{:S(2)}) copy-start(f32[512]{0:T(512)S(1)} %exponential_multiply_fusion) | copy-start | bytes 6148
  51.9 102.0 %copy-start.20 = (f32[1024]{0:T(1024)}, f32[1024]{0:T(1024)S(1)}, u32[]{:S(2)}) copy-start(f32[1024]{0:T(1024)S(1)} %get-tuple-element.34) | copy-start | bytes 12292
  54.3 4.9 %collective-permute-start.3 = (bf16[3,1,1,8,25,128]{5,4,3,2,1,0:T(8,128)(2,1)S(1)}, bf16[3,1,1,8,25,128]{5,4,3,2,1,0:T(8,128)(2,1)S(1)}, u32[]{:S(2)}, u32[]{:S(2)}) collective-permute-start(bf16[3,1,1,8,25,128]{5,4,3,2,1,0:T(8,128)(2,1)S(1)} %pad_maximum_fusion.3), channel_id=1, source_target_pairs={{2,0},{4,2},{6,4},{0,6},{3,1},{5,3},{7,5},{1,7},{10,8},{12,10},{14... | collective-permute-start | bytes 460808 | tf_op jit(solution)/shard_map/ppermute | solution.py:22
  54.4 8.1 %collective-permute-start.2 = (bf16[3,1,1,8,25,128]{5,4,3,2,1,0:T(8,128)(2,1)S(1)}, bf16[3,1,1,8,25,128]{5,4,3,2,1,0:T(8,128)(2,1)}, u32[]{:S(2)}, u32[]{:S(2)}) collective-permute-start(bf16[3,1,1,8,25,128]{5,4,3,2,1,0:T(8,128)(2,1)S(1)} %pad_maximum_fusion.3), channel_id=1, source_target_pairs={{0,2},{2,4},{4,6},{6,0},{1,3},{3,5},{5,7},{7,1},{8,10},{10,12},{12... | collective-permute-start | bytes 460808 | tf_op jit(solution)/shard_map/ppermute | solution.py:19
  55.6 98.3 %copy-start.1 = (f32[1024,128]{1,0:T(8,128)S(1)}, f32[1024,128]{1,0:T(8,128)}, u32[]{:S(2)}) copy-start(f32[1024,128]{1,0:T(8,128)} %param.26) | copy-start | bytes 1572868
  63.6 149.3 %collective-permute-start.5 = (bf16[3,3,1,8,25,128]{5,3,4,2,1,0:T(8,128)(2,1)S(1)}, bf16[3,3,1,8,25,128]{5,3,4,2,1,0:T(8,128)(2,1)}, u32[]{:S(2)}, u32[]{:S(2)}) collective-permute-start(bf16[3,3,1,8,25,128]{5,3,4,2,1,0:T(8,128)(2,1)S(1)} %copy.50), channel_id=1, source_target_pairs={{1,0},{0,1},{3,2},{2,3},{5,4},{4,5},{7,6},{6,7},{9,8},{8,9},{11,10... | collective-permute-start | bytes 1382408 | tf_op jit(solution)/shard_map/ppermute | solution.py:22
  64.1 150.0 %collective-permute-start.4 = (bf16[3,3,1,8,25,128]{5,3,4,2,1,0:T(8,128)(2,1)S(1)}, bf16[3,3,1,8,25,128]{5,3,4,2,1,0:T(8,128)(2,1)S(1)}, u32[]{:S(2)}, u32[]{:S(2)}) collective-permute-start(bf16[3,3,1,8,25,128]{5,3,4,2,1,0:T(8,128)(2,1)S(1)} %copy.50), channel_id=1, source_target_pairs={{0,1},{1,0},{2,3},{3,2},{4,5},{5,4},{6,7},{7,6},{8,9},{9,8},{10,11... | collective-permute-start | bytes 1382408 | tf_op jit(solution)/shard_map/ppermute | solution.py:19
  255.6 5.2 %copy-start.28 = (f32[512]{0:T(512)S(1)}, f32[512]{0:T(512)}, u32[]{:S(2)}) copy-start(f32[512]{0:T(512)} %get-tuple-element.71) | copy-start | bytes 6148
  255.6 5.2 %copy-start.29 = (f32[512]{0:T(512)S(1)}, f32[512]{0:T(512)}, u32[]{:S(2)}) copy-start(f32[512]{0:T(512)} %get-tuple-element.72) | copy-start | bytes 6148
  264.3 4.2 %copy-start.23 = (f32[16,32]{1,0:T(8,128)S(1)}, f32[16,32]{1,0:T(8,128)}, u32[]{:S(2)}) copy-start(f32[16,32]{1,0:T(8,128)} %get-tuple-element.67) | copy-start | bytes 6148
  265.9 6.1 %copy-start.17 = (f32[1,1,1,16,25,128]{5,3,4,2,1,0:T(8,128)S(1)}, f32[1,1,1,16,25,128]{5,3,4,2,1,0:T(8,128)}, u32[]{:S(2)}) copy-start(f32[1,1,1,16,25,128]{5,3,4,2,1,0:T(8,128)} %constant_dynamic-update-slice_fusion.22) | copy-start | bytes 614404
  265.9 6.4 %copy-start.16 = (bf16[1,1,1,16,25,128]{5,3,4,2,1,0:T(8,128)(2,1)S(1)}, bf16[1,1,1,16,25,128]{5,3,4,2,1,0:T(8,128)(2,1)}, u32[]{:S(2)}) copy-start(bf16[1,1,1,16,25,128]{5,3,4,2,1,0:T(8,128)(2,1)} %param.17) | copy-start | bytes 307204
  268.5 4.4 %copy-start.21 = (f32[1024]{0:T(1024)S(1)}, f32[1024]{0:T(1024)}, u32[]{:S(2)}) copy-start(f32[1024]{0:T(1024)} %copy-done.20) | copy-start | bytes 12292
  268.5 4.4 %copy-start.26 = (f32[128]{0:T(128)S(1)}, f32[128]{0:T(128)}, u32[]{:S(2)}) copy-start(f32[128]{0:T(128)} %broadcast_multiply_fusion) | copy-start | bytes 1540
  268.5 6.0 %copy-start.18 = (f32[1,1,1,16,128]{4,3,2,1,0:T(8,128)S(1)}, f32[1,1,1,16,128]{4,3,2,1,0:T(8,128)}, u32[]{:S(2)}) copy-start(f32[1,1,1,16,128]{4,3,2,1,0:T(8,128)} %param.27) | copy-start | bytes 24580
  272.3 4.8 %copy-start.9 = (f32[16,1024]{1,0:T(8,128)S(1)}, f32[16,1024]{1,0:T(8,128)}, u32[]{:S(2)}) copy-start(f32[16,1024]{1,0:T(8,128)} %copy-done.8) | copy-start | bytes 196612
  (18 other events, 52.0 us)
Sparse Core Ops, SparseCore 0:
  21.2 132.6 all-reduce.8
  157.1 55.7 all-reduce.10
  215.4 51.2 all-reduce.12
